TPU v7x, 32 devices: a whole 2x2x4 slice. The times are simulated.
32 devices in a mesh: section: 4 (over y, x), dp: 8 (over z, core).
Axes of the slice: x: 2, y: 2, z: 4, core: 2. Of those that a mesh axis runs over, the one named last changes fastest.
Arguments:
- images: bfloat16 [4, 8, 8, 16, 768], P(None, 'dp'), may hold values from -6 to 6
- widths: int32 [4], replicated, may hold values from 0 to 2, as said below
- depth_kernel: bfloat16 [4, 7, 7, 768], P('section'), may hold values from -0.875 to 0.875
- depth_bias: bfloat16 [4, 768], P('section'), may hold values from -3 to 3
- ln_gain: bfloat16 [4, 768], P('section'), may hold values from 0.25 to 1.75
- ln_bias: bfloat16 [4, 768], P('section'), may hold values from -3 to 3
- w_in: bfloat16 [4, 1536, 768], P('section', 'dp'), may hold values from -0.21875 to 0.21875
- w_out: bfloat16 [4, 1536, 768], P('section', 'dp'), may hold values from -0.15625 to 0.15625
- layer_scale: bfloat16 [4, 768], P('section'), may hold values from 0.29882812 to 1
Outputs:
- section_acts: bfloat16 [4, 4, 8, 8, 16, 768], P('section', None, 'dp')
Inputs may be any that keep to these rules, and one draw needn't show every extreme that they name: `widths`: each half of the micro-batches holds exactly one at level 0 and one at a level above 0; levels 1 and 2 both appear.
All inputs are finite; a program needn't handle non-finite values.
Results may differ from a plain program's by a relative error of at most 0.0065.
Values may be sent and summed in bfloat16 or wider, within the bound.
A program may use at most 64 MiB of HBM per device.

v0:
```python
import jax
import jax.numpy as jnp
from jax import lax
from jax.sharding import PartitionSpec as P


def swapped(value, axis, stride):
    mask = 2**stride
    pairs = [(source, source ^ mask) for source in range(lax.axis_size(axis))]
    return lax.ppermute(value, axis, pairs)


def passed_along(value, axis, steps):
    count = lax.axis_size(axis)
    initial, last = (max(0, -steps), min(count, count - steps))
    return lax.ppermute(value, axis, [(source, source + steps) for source in range(initial, last)])


def conv_block(
    inputs, width_level, depth_kernel, depth_bias, ln_gain, ln_bias, w_in, w_out, layer_scale
):
    channels = inputs.shape[-1]
    hidden = w_in.shape[0]
    active_channels = jnp.where(
        width_level == 0, channels, jnp.where(width_level == 1, channels // 2, channels // 4)
    )
    active_hidden = jnp.where(
        width_level == 0, hidden, jnp.where(width_level == 1, hidden // 2, hidden // 4)
    )
    chan_mask = (jnp.arange(channels) < active_channels).astype(jnp.float32)
    hidden_mask = (jnp.arange(hidden) < active_hidden).astype(jnp.float32)
    channel_count = active_channels.astype(jnp.float32)
    widened = inputs.astype(jnp.float32) * chan_mask
    kernel = depth_kernel.astype(jnp.float32)
    reach = kernel.shape[0] // 2
    padded = jnp.pad(widened, ((0, 0), (reach, reach), (reach, reach), (0, 0)))
    rows_n = inputs.shape[1]
    cols_n = inputs.shape[2]
    spatial = jnp.zeros(widened.shape, jnp.float32)
    for row_off in range(kernel.shape[0]):
        for col_off in range(kernel.shape[1]):
            spatial = (
                spatial
                + padded[:, row_off : row_off + rows_n, col_off : col_off + cols_n, :]
                * kernel[row_off, col_off]
            )
    spatial = (spatial + depth_bias.astype(jnp.float32)) * chan_mask
    average = jnp.sum(spatial, axis=-1, keepdims=True) / channel_count
    centred = (spatial - average) * chan_mask
    variance = jnp.sum(centred * centred, axis=-1, keepdims=True) / channel_count
    normed = (
        centred * lax.rsqrt(variance + 1e-06) * ln_gain.astype(jnp.float32)
        + ln_bias.astype(jnp.float32)
    ) * chan_mask
    flattened = normed.astype(jnp.bfloat16).reshape(-1, channels)
    expanded = jnp.dot(flattened, w_in.T, preferred_element_type=jnp.float32)
    activated = (jax.nn.gelu(expanded, approximate=True) * hidden_mask).astype(jnp.bfloat16)
    projected = jnp.dot(activated, w_out, preferred_element_type=jnp.float32).reshape(widened.shape)
    result = widened + layer_scale.astype(jnp.float32) * projected * chan_mask
    return result.astype(jnp.bfloat16)


def run_slot(
    stored, received, tick_index, offset, entry_first, base_slot, count, images, widths, parameters
):
    slot_index = tick_index - offset
    is_live = (slot_index >= 0) & (slot_index < count)
    clipped = jnp.clip(slot_index, 0, count - 1) + base_slot
    entering = lax.dynamic_index_in_dim(images, clipped, 0, keepdims=False)
    source = jnp.where(entry_first, entering, received)
    width_level = widths[clipped]
    result = lax.cond(
        is_live,
        lambda operand: conv_block(operand, width_level, *parameters),
        lambda operand: jnp.zeros_like(operand),
        source,
    )
    previous = lax.dynamic_index_in_dim(stored, clipped, 0, keepdims=False)
    stored = lax.dynamic_update_index_in_dim(
        stored, jnp.where(is_live, result, previous), clipped, 0
    )
    return (stored, result)


def on_device(images, widths, depth_kernel, depth_bias, ln_gain, ln_bias, w_in, w_out, layer_scale):
    sections = lax.axis_size("section")
    position = lax.axis_index("section")
    microbatches = images.shape[0]
    halfway = microbatches // 2
    bit_total = sections.bit_length() - 1
    stored = jnp.zeros(images.shape, jnp.bfloat16)
    empty_tile = jnp.zeros(images.shape[1:], jnp.bfloat16)
    shards = (w_in, w_out, depth_kernel, depth_bias, ln_gain, ln_bias, layer_scale)
    for bit_index in range(bit_total):
        shards = swapped(
            (shards[0], shards[1], shards[2], shards[3], shards[4], shards[5], shards[6]),
            "section",
            bit_index,
        )
    full_in, full_out, mirror_in, mirror_out = (
        lax.all_gather(w_in, "dp", axis=1, tiled=True),
        lax.all_gather(w_out, "dp", axis=1, tiled=True),
        lax.all_gather(shards[0], "dp", axis=1, tiled=True),
        lax.all_gather(shards[1], "dp", axis=1, tiled=True),
    )
    own_params = (
        depth_kernel[0],
        depth_bias[0],
        ln_gain[0],
        ln_bias[0],
        full_in[0],
        full_out[0],
        layer_scale[0],
    )
    mirror_params = (
        shards[2][0],
        shards[3][0],
        shards[4][0],
        shards[5][0],
        mirror_in[0],
        mirror_out[0],
        shards[6][0],
    )
    tick_total = sections - 1 + halfway

    def advance(tick_index, carried):
        down_received, up_received, kept = carried
        kept, down_result = run_slot(
            kept,
            down_received,
            tick_index,
            position,
            position == 0,
            0,
            halfway,
            images,
            widths,
            own_params,
        )
        kept, up_result = run_slot(
            kept,
            up_received,
            tick_index,
            sections - 1 - position,
            position == sections - 1,
            halfway,
            halfway,
            images,
            widths,
            mirror_params,
        )
        down_received = passed_along(down_result, "section", 1)
        up_received = passed_along(up_result, "section", -1)
        return (down_received, up_received, kept)

    _, _, stored = lax.fori_loop(0, tick_total, advance, (empty_tile, empty_tile, stored))
    return stored[None]


def solution(mesh):
    placed = (
        P(None, "dp", None, None, None),
        P(),
        P("section", None, None, None),
        P("section", None),
        P("section", None),
        P("section", None),
        P("section", "dp", None),
        P("section", "dp", None),
        P("section", None),
    )
    return jax.shard_map(
        on_device,
        mesh=mesh,
        in_specs=placed,
        out_specs=P("section", None, "dp", None, None, None),
        check_vma=False,
    )
```

profile of v0, /device:TPU:6, one launch (start us, length us, event | category | flops | bytes accessed | tf_op | source)
XLA Modules:
  0.0 269.6 jit_solution(6992223651188118496)
XLA Ops:
  6.5 0.7 all-gather.5.cloned.1.call-update
  8.7 8.4 %collective-permute-done.12 = bf16[1,192,768]{2,1,0:T(8,128)(2,1)S(1)} collective-permute-done((bf16[1,192,768]{2,1,0:T(8,128)(2,1)}, bf16[1,192,768]{2,1,0:T(8,128)(2,1)S(1)}, u32[]{:S(2)}, u32[]{:S(2)}) %collective-permute-start.12) | collective-permute-done | bytes 294944 | tf_op jit(solution)/shard_map/ppermute | solution.py:10
  17.6 7.4 %collective-permute-done.13 = bf16[1,192,768]{2,1,0:T(8,128)(2,1)S(1)} collective-permute-done((bf16[1,192,768]{2,1,0:T(8,128)(2,1)S(1)}, bf16[1,192,768]{2,1,0:T(8,128)(2,1)S(1)}, u32[]{:S(2)}, u32[]{:S(2)}) %collective-permute-start.13) | collective-permute-done | bytes 294944 | tf_op jit(solution)/shard_map/ppermute | solution.py:10
  25.0 0.7 copy-done.3
  26.4 6.8 %collective-permute-done.14 = bf16[1,192,768]{2,1,0:T(8,128)(2,1)S(1)} collective-permute-done((bf16[1,192,768]{2,1,0:T(8,128)(2,1)}, bf16[1,192,768]{2,1,0:T(8,128)(2,1)S(1)}, u32[]{:S(2)}, u32[]{:S(2)}) %collective-permute-start.14) | collective-permute-done | bytes 294944 | tf_op jit(solution)/shard_map/ppermute | solution.py:10
  33.7 6.2 %collective-permute-done.15 = bf16[1,192,768]{2,1,0:T(8,128)(2,1)S(1)} collective-permute-done((bf16[1,192,768]{2,1,0:T(8,128)(2,1)S(1)}, bf16[1,192,768]{2,1,0:T(8,128)(2,1)S(1)}, u32[]{:S(2)}, u32[]{:S(2)}) %collective-permute-start.15) | collective-permute-done | bytes 294944 | tf_op jit(solution)/shard_map/ppermute | solution.py:10
  41.2 4.2 %collective-permute-done.4 = bf16[1,7,7,768]{3,2,1,0:T(8,128)(2,1)S(1)} collective-permute-done((bf16[1,7,7,768]{3,2,1,0:T(8,128)(2,1)}, bf16[1,7,7,768]{3,2,1,0:T(8,128)(2,1)S(1)}, u32[]{:S(2)}, u32[]{:S(2)}) %collective-permute-start.4) | collective-permute-done | bytes 75296 | tf_op jit(solution)/shard_map/ppermute | solution.py:10
  46.0 0.8 collective-permute-start.2
  46.8 1.2 collective-permute-start.6
  48.0 0.8 collective-permute-start.8
  48.8 1.2 collective-permute-start.10
  50.0 1.5 collective-permute-start.3
  52.1 1.5 collective-permute-start.9
  57.2 16.8 %all-gather.7.cloned.1.call-done = bf16[1,1536,768]{2,1,0:T(8,128)(2,1)} async-done(((bf16[1,192,768]{2,1,0:T(8,128)(2,1)}), bf16[1,1536,768]{2,1,0:T(8,128)(2,1)}) %all-gather.7.cloned.1.call-update) | async-done | bytes 2359312 | tf_op jit(solution)/shard_map/all_gather | solution.py:102
  74.0 32.4 %all-gather.9.cloned.1.call-done = bf16[1,1536,768]{2,1,0:T(8,128)(2,1)} async-done(((bf16[1,192,768]{2,1,0:T(8,128)(2,1)}), bf16[1,1536,768]{2,1,0:T(8,128)(2,1)}) %all-gather.9.cloned.1.call-update) | async-done | bytes 2359312 | tf_op jit(solution)/shard_map/all_gather | solution.py:103
  106.4 32.2 %all-gather.11.cloned.1.call-done = bf16[1,1536,768]{2,1,0:T(8,128)(2,1)} async-done(((bf16[1,192,768]{2,1,0:T(8,128)(2,1)}), bf16[1,1536,768]{2,1,0:T(8,128)(2,1)}) %all-gather.11.cloned.1.call-update) | async-done | bytes 2359312 | tf_op jit(solution)/shard_map/all_gather | solution.py:104
  138.7 123.5 %while.19 = (s32[]{:T(128)}, bf16[1,8,16,768]{3,2,1,0:T(8,128)(2,1)S(1)}, bf16[1,8,16,768]{3,2,1,0:T(8,128)(2,1)S(1)}, bf16[4,1,8,16,768]{4,3,2,1,0:T(8,128)(2,1...) while((s32[]{:T(128)}, ...), condition=%wide.region_9.10_spmd, body=%wide.region_0.9_spmd.sunk | while | flops 1235378944 | bytes 22721452 | solution.py:156
  138.8 10.3 %conditional.5 = (bf16[1,8,16,768]{3,2,1,0:T(8,128)(2,1)S(1)}) conditional(s32[]{:T(128)} %convert_element_type.176, () %tuple.160, (pred[]{:T(512)}, bf16[4,1,8,16,768]{4,3,2,1,0:T(8,128)(2,1)S(1)}, s32[]{:T(128)}, bf16[1,8,16,768]{3,2,1,0:T(8,128)(2,1)S(1)}, s32[4]{0:T(128)S(1)}, /*index=5*/bf16[768]{0:T(1024)(128)(2,1)S(1)}, ...), branch_computations={%region_5.5_spmd, %region_6.8_spmd} | conditional | flops 617591168 | bytes 9590903 | solution.py:72
  141.4 3.5 %fusion.242 = (f32[8,16]{1,0:T(8,128)S(1)}, f32[1,8,16,768]{3,2,1,0:T(8,128)S(1)}) fusion(f32[768]{0:T(1024)S(1)} %fusion.235, f32[768]{0:T(1024)S(1)} %convert_element_type.149, f32[768]{0:T(1024)S(1)} %get-tuple-element.768, f32[768]{0:T(1024)S(1)} %get-tuple-element.769, f32[768]{0:T(1024)S(1)} %get-tuple-element.770, f32[768]{0:T(1024)S(1)} %get-tuple-element.771, ...), kind=kLoop, calls=%fused_computation.461 | loop fusion | flops 9830272 | bytes 943616 | tf_op jit(solution)/shard_map/while/body/eval_jaxpr/cond/branch_1_fun/reduce_sum | solution.py:48
  145.3 3.7 %fusion.129 = f32[128,768]{1,0:T(8,128)S(1)} fusion(bf16[1536,768]{1,0:T(8,128)(2,1)} %get-tuple-element.690, f32[1536]{0:T(1024)S(1)} %fusion.234, bf16[128,768]{1,0:T(8,128)(2,1)S(1)} %bitcast.51, bf16[1536,768]{1,0:T(8,128)(2,1)} %get-tuple-element.689), kind=kOutput, calls=%fused_computation.285 | convolution fusion | flops 605945856 | bytes 5314560 | tf_op jit(solution)/shard_map/while/body/eval_jaxpr/cond/branch_1_fun/dot_general | solution.py:58
  149.0 1.3 collective-permute-start.1
  150.4 1.3 collective-permute-start
  151.9 3.3 %collective-permute-done.1 = bf16[1,8,16,768]{3,2,1,0:T(8,128)(2,1)S(1)} collective-permute-done((bf16[1,8,16,768]{3,2,1,0:T(8,128)(2,1)S(1)}, bf16[1,8,16,768]{3,2,1,0:T(8,128)(2,1)S(1)}, u32[]{:S(2)}, u32[]{:S(2)}) %collective-permute-start.1) | collective-permute-done | bytes 196640 | tf_op jit(solution)/shard_map/while/body/eval_jaxpr/ppermute | solution.py:16
  155.1 4.2 %collective-permute-done = bf16[1,8,16,768]{3,2,1,0:T(8,128)(2,1)S(1)} collective-permute-done((bf16[1,8,16,768]{3,2,1,0:T(8,128)(2,1)S(1)}, bf16[1,8,16,768]{3,2,1,0:T(8,128)(2,1)S(1)}, u32[]{:S(2)}, u32[]{:S(2)}) %collective-permute-start) | collective-permute-done | bytes 196640 | tf_op jit(solution)/shard_map/while/body/eval_jaxpr/ppermute | solution.py:16
  159.3 10.2 %conditional.5 = (bf16[1,8,16,768]{3,2,1,0:T(8,128)(2,1)S(1)}) conditional(s32[]{:T(128)} %convert_element_type.176, () %tuple.160, (pred[]{:T(512)}, bf16[4,1,8,16,768]{4,3,2,1,0:T(8,128)(2,1)S(1)}, s32[]{:T(128)}, bf16[1,8,16,768]{3,2,1,0:T(8,128)(2,1)S(1)}, s32[4]{0:T(128)S(1)}, /*index=5*/bf16[768]{0:T(1024)(128)(2,1)S(1)}, ...), branch_computations={%region_5.5_spmd, %region_6.8_spmd} | conditional | flops 617591168 | bytes 9590903 | solution.py:72
  161.9 3.5 %fusion.242 = (f32[8,16]{1,0:T(8,128)S(1)}, f32[1,8,16,768]{3,2,1,0:T(8,128)S(1)}) fusion(f32[768]{0:T(1024)S(1)} %fusion.235, f32[768]{0:T(1024)S(1)} %convert_element_type.149, f32[768]{0:T(1024)S(1)} %get-tuple-element.768, f32[768]{0:T(1024)S(1)} %get-tuple-element.769, f32[768]{0:T(1024)S(1)} %get-tuple-element.770, f32[768]{0:T(1024)S(1)} %get-tuple-element.771, ...), kind=kLoop, calls=%fused_computation.461 | loop fusion | flops 9830272 | bytes 943616 | tf_op jit(solution)/shard_map/while/body/eval_jaxpr/cond/branch_1_fun/reduce_sum | solution.py:48
  165.8 3.7 %fusion.129 = f32[128,768]{1,0:T(8,128)S(1)} fusion(bf16[1536,768]{1,0:T(8,128)(2,1)} %get-tuple-element.690, f32[1536]{0:T(1024)S(1)} %fusion.234, bf16[128,768]{1,0:T(8,128)(2,1)S(1)} %bitcast.51, bf16[1536,768]{1,0:T(8,128)(2,1)} %get-tuple-element.689), kind=kOutput, calls=%fused_computation.285 | convolution fusion | flops 605945856 | bytes 5314560 | tf_op jit(solution)/shard_map/while/body/eval_jaxpr/cond/branch_1_fun/dot_general | solution.py:58
  169.6 1.5 collective-permute-start.1
  171.1 1.3 collective-permute-start
  172.6 2.2 collective-permute-done.1
  174.8 4.8 %collective-permute-done = bf16[1,8,16,768]{3,2,1,0:T(8,128)(2,1)S(1)} collective-permute-done((bf16[1,8,16,768]{3,2,1,0:T(8,128)(2,1)S(1)}, bf16[1,8,16,768]{3,2,1,0:T(8,128)(2,1)S(1)}, u32[]{:S(2)}, u32[]{:S(2)}) %collective-permute-start) | collective-permute-done | bytes 196640 | tf_op jit(solution)/shard_map/while/body/eval_jaxpr/ppermute | solution.py:16
  179.7 12.5 %collective-permute-start.1 = (bf16[1,8,16,768]{3,2,1,0:T(8,128)(2,1)S(1)}, bf16[1,8,16,768]{3,2,1,0:T(8,128)(2,1)S(1)}, u32[]{:S(2)}, u32[]{:S(2)}) collective-permute-start(bf16[1,8,16,768]{3,2,1,0:T(8,128)(2,1)S(1)} %get-tuple-element.1098), channel_id=1, source_target_pairs={{8,0},{16,8},{24,16},{9,1},{17,9},{25,17},{10,2},{18,10},{26,18},{... | collective-permute-start | bytes 589832 | tf_op jit(solution)/shard_map/while/body/eval_jaxpr/ppermute | solution.py:16
  192.3 1.3 collective-permute-start
  193.8 1.6 collective-permute-done.1
  195.4 12.6 %collective-permute-done = bf16[1,8,16,768]{3,2,1,0:T(8,128)(2,1)S(1)} collective-permute-done((bf16[1,8,16,768]{3,2,1,0:T(8,128)(2,1)S(1)}, bf16[1,8,16,768]{3,2,1,0:T(8,128)(2,1)S(1)}, u32[]{:S(2)}, u32[]{:S(2)}) %collective-permute-start) | collective-permute-done | bytes 196640 | tf_op jit(solution)/shard_map/while/body/eval_jaxpr/ppermute | solution.py:16
  208.0 4.8 %collective-permute-start.1 = (bf16[1,8,16,768]{3,2,1,0:T(8,128)(2,1)S(1)}, bf16[1,8,16,768]{3,2,1,0:T(8,128)(2,1)S(1)}, u32[]{:S(2)}, u32[]{:S(2)}) collective-permute-start(bf16[1,8,16,768]{3,2,1,0:T(8,128)(2,1)S(1)} %get-tuple-element.1098), channel_id=1, source_target_pairs={{8,0},{16,8},{24,16},{9,1},{17,9},{25,17},{10,2},{18,10},{26,18},{... | collective-permute-start | bytes 589832 | tf_op jit(solution)/shard_map/while/body/eval_jaxpr/ppermute | solution.py:16
  212.9 10.2 %conditional.4 = (bf16[1,8,16,768]{3,2,1,0:T(8,128)(2,1)S(1)}) conditional(s32[]{:T(128)} %convert_element_type.175, () %tuple.158, (pred[]{:T(512)}, bf16[4,1,8,16,768]{4,3,2,1,0:T(8,128)(2,1)S(1)}, s32[]{:T(128)}, bf16[1,8,16,768]{3,2,1,0:T(8,128)(2,1)S(1)}, s32[4]{0:T(128)S(1)}, /*index=5*/bf16[768]{0:T(1024)(128)(2,1)S(1)}, ...), branch_computations={%region_1.1_spmd, %region_2.4_spmd} | conditional | flops 617591168 | bytes 9590903 | solution.py:72
  215.4 3.5 %fusion.240 = (f32[8,16]{1,0:T(8,128)S(1)}, f32[1,8,16,768]{3,2,1,0:T(8,128)S(1)}) fusion(f32[768]{0:T(1024)S(1)} %fusion.115, f32[768]{0:T(1024)S(1)} %convert_element_type.137, f32[768]{0:T(1024)S(1)} %get-tuple-element.719, f32[768]{0:T(1024)S(1)} %get-tuple-element.720, f32[768]{0:T(1024)S(1)} %get-tuple-element.721, f32[768]{0:T(1024)S(1)} %get-tuple-element.722, ...), kind=kLoop, calls=%fused_computation.460 | loop fusion | flops 9830272 | bytes 943616 | tf_op jit(solution)/shard_map/while/body/eval_jaxpr/cond/branch_1_fun/reduce_sum | solution.py:48
  219.3 3.7 %fusion.9 = f32[128,768]{1,0:T(8,128)S(1)} fusion(bf16[1536,768]{1,0:T(8,128)(2,1)} %get-tuple-element.678, f32[1536]{0:T(1024)S(1)} %fusion.114, bf16[128,768]{1,0:T(8,128)(2,1)S(1)} %bitcast.52, bf16[1536,768]{1,0:T(8,128)(2,1)} %get-tuple-element.677), kind=kOutput, calls=%fused_computation.58 | convolution fusion | flops 605945856 | bytes 5314560 | tf_op jit(solution)/shard_map/while/body/eval_jaxpr/cond/branch_1_fun/dot_general | solution.py:58
  223.1 1.3 collective-permute-start
  224.6 13.8 %collective-permute-done = bf16[1,8,16,768]{3,2,1,0:T(8,128)(2,1)S(1)} collective-permute-done((bf16[1,8,16,768]{3,2,1,0:T(8,128)(2,1)S(1)}, bf16[1,8,16,768]{3,2,1,0:T(8,128)(2,1)S(1)}, u32[]{:S(2)}, u32[]{:S(2)}) %collective-permute-start) | collective-permute-done | bytes 196640 | tf_op jit(solution)/shard_map/while/body/eval_jaxpr/ppermute | solution.py:16
  238.4 6.0 %collective-permute-start.1 = (bf16[1,8,16,768]{3,2,1,0:T(8,128)(2,1)S(1)}, bf16[1,8,16,768]{3,2,1,0:T(8,128)(2,1)S(1)}, u32[]{:S(2)}, u32[]{:S(2)}) collective-permute-start(bf16[1,8,16,768]{3,2,1,0:T(8,128)(2,1)S(1)} %get-tuple-element.1098), channel_id=1, source_target_pairs={{8,0},{16,8},{24,16},{9,1},{17,9},{25,17},{10,2},{18,10},{26,18},{... | collective-permute-start | bytes 589832 | tf_op jit(solution)/shard_map/while/body/eval_jaxpr/ppermute | solution.py:16
  244.4 10.2 %conditional.4 = (bf16[1,8,16,768]{3,2,1,0:T(8,128)(2,1)S(1)}) conditional(s32[]{:T(128)} %convert_element_type.175, () %tuple.158, (pred[]{:T(512)}, bf16[4,1,8,16,768]{4,3,2,1,0:T(8,128)(2,1)S(1)}, s32[]{:T(128)}, bf16[1,8,16,768]{3,2,1,0:T(8,128)(2,1)S(1)}, s32[4]{0:T(128)S(1)}, /*index=5*/bf16[768]{0:T(1024)(128)(2,1)S(1)}, ...), branch_computations={%region_1.1_spmd, %region_2.4_spmd} | conditional | flops 617591168 | bytes 9590903 | solution.py:72
  246.9 3.5 %fusion.240 = (f32[8,16]{1,0:T(8,128)S(1)}, f32[1,8,16,768]{3,2,1,0:T(8,128)S(1)}) fusion(f32[768]{0:T(1024)S(1)} %fusion.115, f32[768]{0:T(1024)S(1)} %convert_element_type.137, f32[768]{0:T(1024)S(1)} %get-tuple-element.719, f32[768]{0:T(1024)S(1)} %get-tuple-element.720, f32[768]{0:T(1024)S(1)} %get-tuple-element.721, f32[768]{0:T(1024)S(1)} %get-tuple-element.722, ...), kind=kLoop, calls=%fused_computation.460 | loop fusion | flops 9830272 | bytes 943616 | tf_op jit(solution)/shard_map/while/body/eval_jaxpr/cond/branch_1_fun/reduce_sum | solution.py:48
  250.9 3.7 %fusion.9 = f32[128,768]{1,0:T(8,128)S(1)} fusion(bf16[1536,768]{1,0:T(8,128)(2,1)} %get-tuple-element.678, f32[1536]{0:T(1024)S(1)} %fusion.114, bf16[128,768]{1,0:T(8,128)(2,1)S(1)} %bitcast.52, bf16[1536,768]{1,0:T(8,128)(2,1)} %get-tuple-element.677), kind=kOutput, calls=%fused_computation.58 | convolution fusion | flops 605945856 | bytes 5314560 | tf_op jit(solution)/shard_map/while/body/eval_jaxpr/cond/branch_1_fun/dot_general | solution.py:58
  254.6 1.3 collective-permute-start
  256.1 6.1 %collective-permute-done = bf16[1,8,16,768]{3,2,1,0:T(8,128)(2,1)S(1)} collective-permute-done((bf16[1,8,16,768]{3,2,1,0:T(8,128)(2,1)S(1)}, bf16[1,8,16,768]{3,2,1,0:T(8,128)(2,1)S(1)}, u32[]{:S(2)}, u32[]{:S(2)}) %collective-permute-start) | collective-permute-done | bytes 196640 | tf_op jit(solution)/shard_map/while/body/eval_jaxpr/ppermute | solution.py:16
  262.2 0.9 copy-done
  (148 shorter events, 16.7 us)
Async XLA Ops:
  6.5 132.2 %copy-start.2 = (bf16[1,7,7,768]{3,2,1,0:T(8,128)(2,1)S(1)}, bf16[1,7,7,768]{3,2,1,0:T(8,128)(2,1)}, u32[]{:S(2)}) copy-start(bf16[1,7,7,768]{3,2,1,0:T(8,128)(2,1)} %param.17) | copy-start | bytes 225796
  6.5 132.2 %copy-start.1 = (bf16[4,1,8,16,768]{4,3,2,1,0:T(8,128)(2,1)S(1)}, bf16[4,1,8,16,768]{4,3,2,1,0:T(8,128)(2,1)}, u32[]{:S(2)}) copy-start(bf16[4,1,8,16,768]{4,3,2,1,0:T(8,128)(2,1)} %param.15) | copy-start | bytes 2359300
  6.5 132.2 %copy-start.5 = (s32[4]{0:T(128)S(1)}, s32[4]{0:T(128)}, u32[]{:S(2)}) copy-start(s32[4]{0:T(128)} %param.16) | copy-start | bytes 52
  6.5 50.7 %all-gather.5.cloned.1.call-start = ((), (), s32[]{:S(2)}) async-start(), calls=%async_computation | async-start | bytes 2654208 | tf_op jit(solution)/shard_map/all_gather | solution.py:101
  7.3 66.7 %all-gather.7.cloned.1.call-start = ((), (), s32[]{:S(2)}) async-start(), calls=%async_computation.1 | async-start | bytes 2654208 | tf_op jit(solution)/shard_map/all_gather | solution.py:102
  8.0 98.4 %all-gather.9.cloned.1.call-start = ((), (), s32[]{:S(2)}) async-start(), calls=%async_computation.2 | async-start | bytes 2654208 | tf_op jit(solution)/shard_map/all_gather | solution.py:103
  8.1 9.0 %collective-permute-start.12 = (bf16[1,192,768]{2,1,0:T(8,128)(2,1)}, bf16[1,192,768]{2,1,0:T(8,128)(2,1)S(1)}, u32[]{:S(2)}, u32[]{:S(2)}) collective-permute-start(bf16[1,192,768]{2,1,0:T(8,128)(2,1)} %param.21), channel_id=1, source_target_pairs={{0,8},{8,0},{16,24},{24,16},{1,9},{9,1},{17,25},{25,17},{2,10},{10... | collective-permute-start | bytes 884744 | tf_op jit(solution)/shard_map/ppermute | solution.py:10
  17.1 7.9 %collective-permute-start.13 = (bf16[1,192,768]{2,1,0:T(8,128)(2,1)S(1)}, bf16[1,192,768]{2,1,0:T(8,128)(2,1)S(1)}, u32[]{:S(2)}, u32[]{:S(2)}) collective-permute-start(bf16[1,192,768]{2,1,0:T(8,128)(2,1)S(1)} %collective-permute-done.12), channel_id=1, source_target_pairs={{0,16},{8,24},{16,0},{24,8},{1,17},{9,25},{17,1},{25,9},{2,18},{10... | collective-permute-start | bytes 884744 | tf_op jit(solution)/shard_map/ppermute | solution.py:10
  25.0 0.7 copy-start.3
  25.7 112.9 %all-gather.11.cloned.1.call-start = ((), (), s32[]{:S(2)}) async-start(), calls=%async_computation.3 | async-start | bytes 2654208 | tf_op jit(solution)/shard_map/all_gather | solution.py:104
  25.8 7.4 %collective-permute-start.14 = (bf16[1,192,768]{2,1,0:T(8,128)(2,1)}, bf16[1,192,768]{2,1,0:T(8,128)(2,1)S(1)}, u32[]{:S(2)}, u32[]{:S(2)}) collective-permute-start(bf16[1,192,768]{2,1,0:T(8,128)(2,1)} %param.22), channel_id=1, source_target_pairs={{0,8},{8,0},{16,24},{24,16},{1,9},{9,1},{17,25},{25,17},{2,10},{10... | collective-permute-start | bytes 884744 | tf_op jit(solution)/shard_map/ppermute | solution.py:10
  33.2 6.7 %collective-permute-start.15 = (bf16[1,192,768]{2,1,0:T(8,128)(2,1)S(1)}, bf16[1,192,768]{2,1,0:T(8,128)(2,1)S(1)}, u32[]{:S(2)}, u32[]{:S(2)}) collective-permute-start(bf16[1,192,768]{2,1,0:T(8,128)(2,1)S(1)} %collective-permute-done.14), channel_id=1, source_target_pairs={{0,16},{8,24},{16,0},{24,8},{1,17},{9,25},{17,1},{25,9},{2,18},{10... | collective-permute-start | bytes 884744 | tf_op jit(solution)/shard_map/ppermute | solution.py:10
  39.9 0.7 copy-start.4
  40.6 4.8 %collective-permute-start.4 = (bf16[1,7,7,768]{3,2,1,0:T(8,128)(2,1)}, bf16[1,7,7,768]{3,2,1,0:T(8,128)(2,1)S(1)}, u32[]{:S(2)}, u32[]{:S(2)}) collective-permute-start(bf16[1,7,7,768]{3,2,1,0:T(8,128)(2,1)} %param.17), channel_id=1, source_target_pairs={{0,8},{8,0},{16,24},{24,16},{1,9},{9,1},{17,25},{25,17},{2,10},{10... | collective-permute-start | bytes 225800 | tf_op jit(solution)/shard_map/ppermute | solution.py:10
  45.4 11.7 %collective-permute-start.5 = (bf16[1,7,7,768]{3,2,1,0:T(8,128)(2,1)S(1)}, bf16[1,7,7,768]{3,2,1,0:T(8,128)(2,1)S(1)}, u32[]{:S(2)}, u32[]{:S(2)}) collective-permute-start(bf16[1,7,7,768]{3,2,1,0:T(8,128)(2,1)S(1)} %collective-permute-done.4), channel_id=1, source_target_pairs={{0,16},{8,24},{16,0},{24,8},{1,17},{9,25},{17,1},{25,9},{2,18},{10... | collective-permute-start | bytes 225800 | tf_op jit(solution)/shard_map/ppermute | solution.py:10
  46.0 4.1 %collective-permute-start.2 = (bf16[1,768]{1,0:T(2,128)(2,1)}, bf16[1,768]{1,0:T(2,128)(2,1)S(1)}, u32[]{:S(2)}, u32[]{:S(2)}) collective-permute-start(bf16[1,768]{1,0:T(2,128)(2,1)} %param.23), channel_id=1, source_target_pairs={{0,8},{8,0},{16,24},{24,16},{1,9},{9,1},{17,25},{25,17},{2,10},{10... | collective-permute-start | bytes 4616 | tf_op jit(solution)/shard_map/ppermute | solution.py:10
  46.8 4.7 %collective-permute-start.6 = (bf16[1,768]{1,0:T(2,128)(2,1)}, bf16[1,768]{1,0:T(2,128)(2,1)S(1)}, u32[]{:S(2)}, u32[]{:S(2)}) collective-permute-start(bf16[1,768]{1,0:T(2,128)(2,1)} %param.18), channel_id=1, source_target_pairs={{0,8},{8,0},{16,24},{24,16},{1,9},{9,1},{17,25},{25,17},{2,10},{10... | collective-permute-start | bytes 4616 | tf_op jit(solution)/shard_map/ppermute | solution.py:10
  48.0 4.1 %collective-permute-start.8 = (bf16[1,768]{1,0:T(2,128)(2,1)}, bf16[1,768]{1,0:T(2,128)(2,1)S(1)}, u32[]{:S(2)}, u32[]{:S(2)}) collective-permute-start(bf16[1,768]{1,0:T(2,128)(2,1)} %param.19), channel_id=1, source_target_pairs={{0,8},{8,0},{16,24},{24,16},{1,9},{9,1},{17,25},{25,17},{2,10},{10... | collective-permute-start | bytes 4616 | tf_op jit(solution)/shard_map/ppermute | solution.py:10
  48.8 4.7 %collective-permute-start.10 = (bf16[1,768]{1,0:T(2,128)(2,1)}, bf16[1,768]{1,0:T(2,128)(2,1)S(1)}, u32[]{:S(2)}, u32[]{:S(2)}) collective-permute-start(bf16[1,768]{1,0:T(2,128)(2,1)} %param.20), channel_id=1, source_target_pairs={{0,8},{8,0},{16,24},{24,16},{1,9},{9,1},{17,25},{25,17},{2,10},{10... | collective-permute-start | bytes 4616 | tf_op jit(solution)/shard_map/ppermute | solution.py:10
  50.0 6.9 %collective-permute-start.3 = (bf16[1,768]{1,0:T(2,128)(2,1)S(1)}, bf16[1,768]{1,0:T(2,128)(2,1)S(1)}, u32[]{:S(2)}, u32[]{:S(2)}) collective-permute-start(bf16[1,768]{1,0:T(2,128)(2,1)S(1)} %collective-permute-done.2), channel_id=1, source_target_pairs={{0,16},{8,24},{16,0},{24,8},{1,17},{9,25},{17,1},{25,9},{2,18},{10... | collective-permute-start | bytes 4616 | tf_op jit(solution)/shard_map/ppermute | solution.py:10
  51.5 5.4 %collective-permute-start.7 = (bf16[1,768]{1,0:T(2,128)(2,1)S(1)}, bf16[1,768]{1,0:T(2,128)(2,1)S(1)}, u32[]{:S(2)}, u32[]{:S(2)}) collective-permute-start(bf16[1,768]{1,0:T(2,128)(2,1)S(1)} %collective-permute-done.6), channel_id=1, source_target_pairs={{0,16},{8,24},{16,0},{24,8},{1,17},{9,25},{17,1},{25,9},{2,18},{10... | collective-permute-start | bytes 4616 | tf_op jit(solution)/shard_map/ppermute | solution.py:10
  52.1 4.9 %collective-permute-start.9 = (bf16[1,768]{1,0:T(2,128)(2,1)S(1)}, bf16[1,768]{1,0:T(2,128)(2,1)S(1)}, u32[]{:S(2)}, u32[]{:S(2)}) collective-permute-start(bf16[1,768]{1,0:T(2,128)(2,1)S(1)} %collective-permute-done.8), channel_id=1, source_target_pairs={{0,16},{8,24},{16,0},{24,8},{1,17},{9,25},{17,1},{25,9},{2,18},{10... | collective-permute-start | bytes 4616 | tf_op jit(solution)/shard_map/ppermute | solution.py:10
  53.6 3.6 %collective-permute-start.11 = (bf16[1,768]{1,0:T(2,128)(2,1)S(1)}, bf16[1,768]{1,0:T(2,128)(2,1)S(1)}, u32[]{:S(2)}, u32[]{:S(2)}) collective-permute-start(bf16[1,768]{1,0:T(2,128)(2,1)S(1)} %collective-permute-done.10), channel_id=1, source_target_pairs={{0,16},{8,24},{16,0},{24,8},{1,17},{9,25},{17,1},{25,9},{2,18},{10... | collective-permute-start | bytes 4616 | tf_op jit(solution)/shard_map/ppermute | solution.py:10
  149.0 6.1 %collective-permute-start.1 = (bf16[1,8,16,768]{3,2,1,0:T(8,128)(2,1)S(1)}, bf16[1,8,16,768]{3,2,1,0:T(8,128)(2,1)S(1)}, u32[]{:S(2)}, u32[]{:S(2)}) collective-permute-start(bf16[1,8,16,768]{3,2,1,0:T(8,128)(2,1)S(1)} %get-tuple-element.1098), channel_id=1, source_target_pairs={{8,0},{16,8},{24,16},{9,1},{17,9},{25,17},{10,2},{18,10},{26,18},{... | collective-permute-start | bytes 589832 | tf_op jit(solution)/shard_map/while/body/eval_jaxpr/ppermute | solution.py:16
  150.4 8.9 %collective-permute-start = (bf16[1,8,16,768]{3,2,1,0:T(8,128)(2,1)S(1)}, bf16[1,8,16,768]{3,2,1,0:T(8,128)(2,1)S(1)}, u32[]{:S(2)}, u32[]{:S(2)}) collective-permute-start(bf16[1,8,16,768]{3,2,1,0:T(8,128)(2,1)S(1)} %get-tuple-element.1097), channel_id=1, source_target_pairs={{0,8},{8,16},{16,24},{1,9},{9,17},{17,25},{2,10},{10,18},{18,26},{... | collective-permute-start | bytes 589832 | tf_op jit(solution)/shard_map/while/body/eval_jaxpr/ppermute | solution.py:16
  169.6 5.3 %collective-permute-start.1 = (bf16[1,8,16,768]{3,2,1,0:T(8,128)(2,1)S(1)}, bf16[1,8,16,768]{3,2,1,0:T(8,128)(2,1)S(1)}, u32[]{:S(2)}, u32[]{:S(2)}) collective-permute-start(bf16[1,8,16,768]{3,2,1,0:T(8,128)(2,1)S(1)} %get-tuple-element.1098), channel_id=1, source_target_pairs={{8,0},{16,8},{24,16},{9,1},{17,9},{25,17},{10,2},{18,10},{26,18},{... | collective-permute-start | bytes 589832 | tf_op jit(solution)/shard_map/while/body/eval_jaxpr/ppermute | solution.py:16
  171.1 8.6 %collective-permute-start = (bf16[1,8,16,768]{3,2,1,0:T(8,128)(2,1)S(1)}, bf16[1,8,16,768]{3,2,1,0:T(8,128)(2,1)S(1)}, u32[]{:S(2)}, u32[]{:S(2)}) collective-permute-start(bf16[1,8,16,768]{3,2,1,0:T(8,128)(2,1)S(1)} %get-tuple-element.1097), channel_id=1, source_target_pairs={{0,8},{8,16},{16,24},{1,9},{9,17},{17,25},{2,10},{10,18},{18,26},{... | collective-permute-start | bytes 589832 | tf_op jit(solution)/shard_map/while/body/eval_jaxpr/ppermute | solution.py:16
  179.7 15.7 %collective-permute-start.1 = (bf16[1,8,16,768]{3,2,1,0:T(8,128)(2,1)S(1)}, bf16[1,8,16,768]{3,2,1,0:T(8,128)(2,1)S(1)}, u32[]{:S(2)}, u32[]{:S(2)}) collective-permute-start(bf16[1,8,16,768]{3,2,1,0:T(8,128)(2,1)S(1)} %get-tuple-element.1098), channel_id=1, source_target_pairs={{8,0},{16,8},{24,16},{9,1},{17,9},{25,17},{10,2},{18,10},{26,18},{... | collective-permute-start | bytes 589832 | tf_op jit(solution)/shard_map/while/body/eval_jaxpr/ppermute | solution.py:16
  192.3 15.7 %collective-permute-start = (bf16[1,8,16,768]{3,2,1,0:T(8,128)(2,1)S(1)}, bf16[1,8,16,768]{3,2,1,0:T(8,128)(2,1)S(1)}, u32[]{:S(2)}, u32[]{:S(2)}) collective-permute-start(bf16[1,8,16,768]{3,2,1,0:T(8,128)(2,1)S(1)} %get-tuple-element.1097), channel_id=1, source_target_pairs={{0,8},{8,16},{16,24},{1,9},{9,17},{17,25},{2,10},{10,18},{18,26},{... | collective-permute-start | bytes 589832 | tf_op jit(solution)/shard_map/while/body/eval_jaxpr/ppermute | solution.py:16
  208.0 16.5 %collective-permute-start.1 = (bf16[1,8,16,768]{3,2,1,0:T(8,128)(2,1)S(1)}, bf16[1,8,16,768]{3,2,1,0:T(8,128)(2,1)S(1)}, u32[]{:S(2)}, u32[]{:S(2)}) collective-permute-start(bf16[1,8,16,768]{3,2,1,0:T(8,128)(2,1)S(1)} %get-tuple-element.1098), channel_id=1, source_target_pairs={{8,0},{16,8},{24,16},{9,1},{17,9},{25,17},{10,2},{18,10},{26,18},{... | collective-permute-start | bytes 589832 | tf_op jit(solution)/shard_map/while/body/eval_jaxpr/ppermute | solution.py:16
  223.1 15.3 %collective-permute-start = (bf16[1,8,16,768]{3,2,1,0:T(8,128)(2,1)S(1)}, bf16[1,8,16,768]{3,2,1,0:T(8,128)(2,1)S(1)}, u32[]{:S(2)}, u32[]{:S(2)}) collective-permute-start(bf16[1,8,16,768]{3,2,1,0:T(8,128)(2,1)S(1)} %get-tuple-element.1097), channel_id=1, source_target_pairs={{0,8},{8,16},{16,24},{1,9},{9,17},{17,25},{2,10},{10,18},{18,26},{... | collective-permute-start | bytes 589832 | tf_op jit(solution)/shard_map/while/body/eval_jaxpr/ppermute | solution.py:16
  238.4 17.7 %collective-permute-start.1 = (bf16[1,8,16,768]{3,2,1,0:T(8,128)(2,1)S(1)}, bf16[1,8,16,768]{3,2,1,0:T(8,128)(2,1)S(1)}, u32[]{:S(2)}, u32[]{:S(2)}) collective-permute-start(bf16[1,8,16,768]{3,2,1,0:T(8,128)(2,1)S(1)} %get-tuple-element.1098), channel_id=1, source_target_pairs={{8,0},{16,8},{24,16},{9,1},{17,9},{25,17},{10,2},{18,10},{26,18},{... | collective-permute-start | bytes 589832 | tf_op jit(solution)/shard_map/while/body/eval_jaxpr/ppermute | solution.py:16
  254.6 7.6 %collective-permute-start = (bf16[1,8,16,768]{3,2,1,0:T(8,128)(2,1)S(1)}, bf16[1,8,16,768]{3,2,1,0:T(8,128)(2,1)S(1)}, u32[]{:S(2)}, u32[]{:S(2)}) collective-permute-start(bf16[1,8,16,768]{3,2,1,0:T(8,128)(2,1)S(1)} %get-tuple-element.1097), channel_id=1, source_target_pairs={{0,8},{8,16},{16,24},{1,9},{9,17},{17,25},{2,10},{10,18},{18,26},{... | collective-permute-start | bytes 589832 | tf_op jit(solution)/shard_map/while/body/eval_jaxpr/ppermute | solution.py:16
  262.2 0.9 copy-start
Sparse Core Ops, SparseCore 0:
  9.0 32.6 all-gather.4
  43.3 30.6 all-gather.6
  75.6 30.6 all-gather.8
  107.9 30.6 all-gather.10
where the time goes:
time: 270 us
  waiting for transfers between devices  165 us (61%)
  starting transfers between devices  44.2 us (16%)
  other arithmetic  19.5 us (7%)
  matrix products  14.7 us (5%)
  between operations  13.2 us (5%)
  local copies, waits for them, and re-layouts  7.06 us (3%)
  loops' own time  6.28 us (2%)
    ppermute x10, waiting for transfers between devices, passed_along(): lax.ppermute(value, axis, [(source, source + steps) for source in range(i...  48.6 us
    ppermute x14, waiting for transfers between devices, swapped(): return lax.ppermute(value, axis, pairs)  33.2 us
    ppermute x10, starting transfers between devices, passed_along(): lax.ppermute(value, axis, [(source, source + steps) for source in range(i...  32.6 us
    all_gather x1, waiting for transfers between devices, on_device(): lax.all_gather(shards[0], 'dp', axis=1, tiled=True)  32.4 us
    all_gather x1, waiting for transfers between devices, on_device(): lax.all_gather(shards[1], 'dp', axis=1, tiled=True)  32.2 us
    all_gather x1, waiting for transfers between devices, on_device(): lax.all_gather(w_out, 'dp', axis=1, tiled=True)  16.8 us
    dot_general x4, matrix products, conv_block(): jnp.dot(activated, w_out, preferred_element_type=jnp.float32)  14.7 us
    reduce_sum x4, other arithmetic, conv_block(): average = jnp.sum(spatial, axis=-1, keepdims=True) / channel_count  13.8 us
  transfers between devices with their start and end apart: 28, of which 17 were waited for; matrix products, arithmetic and copies ran while one was open for 8% of the time, Pallas kernels for 0%

commit v1 on v0

v1 whole, which is shorter than its diff:
```python
import functools

import jax
import jax.numpy as jnp
from jax import lax
from jax.experimental import pallas as pl
from jax.experimental.pallas import tpu as pltpu
from jax.sharding import PartitionSpec as P

MESH = pl.DeviceIdType.MESH
LANES = 128
LEFT = 8


def active_of(level, full):
    return jnp.where(level == 0, full, jnp.where(level == 1, full // 2, full // 4))


def relay_kernel(
    sections,
    shards,
    widths,
    images,
    depth_kernel,
    depth_bias,
    ln_gain,
    ln_bias,
    w_in,
    w_out,
    layer_scale,
    out,
    in_full,
    out_full,
    tiles,
    results,
    padded,
    spatial,
    normed,
    total,
    taps,
    local_sem,
    tile_sem,
    weight_send,
    weight_recv,
    tile_send,
    tile_recv,
    store_send,
    store_recv,
):
    position = lax.axis_index("section")
    rank = lax.axis_index("dp")
    chips = shards // 2
    chip = rank // 2
    core = rank % 2
    sibling = rank + 1 - 2 * core
    mirror = sections - 1 - position
    count, rows_n, cols_n, channels = tiles.shape
    halfway = count // 2
    hidden = in_full.shape[0]
    piece = hidden // shards
    side = depth_kernel.shape[1]
    reach = side // 2
    full = (in_full, out_full)

    def span(shard):
        return pl.ds(pl.multiple_of(shard * piece, 16), piece)

    own = [
        pltpu.make_async_copy(source.at[0], full[kind].at[span(rank)], local_sem.at[kind])
        for kind, source in enumerate((w_in, w_out))
    ]
    for copy in own:
        copy.start()

    def tile_in(slot):
        return pltpu.make_async_copy(images.at[slot, 0], tiles.at[slot], tile_sem.at[slot])

    @pl.when(position == 0)
    def _():
        for slot in range(count):
            tile_in(slot).start()

    barrier = pltpu.get_barrier_semaphore()
    pl.semaphore_signal(barrier, inc=1, device_id={"dp": sibling}, device_id_type=MESH)
    pl.semaphore_signal(barrier, inc=1, device_id={"section": mirror}, device_id_type=MESH)

    def greet(condition, target):
        @pl.when(condition)
        def _():
            pl.semaphore_signal(barrier, inc=1, device_id=target, device_id_type=MESH)

    greet(chip + 1 < chips, {"dp": rank + 2})
    greet(chip > 0, {"dp": rank - 2})
    greet(position + 1 < sections, {"section": position + 1})
    greet(position > 0, {"section": position - 1})

    for row in range(side):
        taps[row, 0:side, :] = depth_kernel[0, row].astype(jnp.float32)
    padded[:, 0:LEFT, :] = jnp.zeros((rows_n, LEFT, channels), jnp.float32)
    padded[:, LEFT + cols_n :, :] = jnp.zeros((rows_n, LEFT, channels), jnp.float32)
    for copy in own:
        copy.wait()

    greeted = 2 + sum(
        jnp.where(condition, 1, 0)
        for condition in (
            chip + 1 < chips,
            chip > 0,
            position + 1 < sections,
            position > 0,
        )
    )
    pl.semaphore_wait(barrier, greeted)

    @pl.when(position == 0)
    def _():
        for slot in range(count):
            tile_in(slot).wait()

    def weight_copy(kind, shard, target, lane, step):
        return pltpu.make_async_remote_copy(
            src_ref=full[kind].at[span(shard)],
            dst_ref=full[kind].at[span(shard)],
            send_sem=weight_send.at[kind, lane, step],
            recv_sem=weight_recv.at[kind, shard],
            device_id={"dp": target},
            device_id_type=MESH,
        )

    def conv_norm(slot):
        level = widths[slot]
        active = active_of(level, channels)
        mask_all = (lax.broadcasted_iota(jnp.int32, (1, channels), 1) < active).astype(jnp.float32)
        for row in range(rows_n):
            padded[row, LEFT : LEFT + cols_n, :] = (
                tiles[slot, row].astype(jnp.float32) * mask_all
            )

        def one_chunk(chunk, carried):
            start = pl.multiple_of(chunk * LANES, LANES)
            lanes = pl.ds(start, LANES)
            sums = [jnp.zeros((cols_n, LANES), jnp.float32) for _ in range(rows_n)]
            for col in range(side):
                rows = [
                    padded[row, pl.ds(LEFT - reach + col, cols_n), lanes] for row in range(rows_n)
                ]
                for row_off in range(side):
                    tap = taps[row_off, pl.ds(col, 1), lanes]
                    for row in range(rows_n):
                        source = row + row_off - reach
                        if 0 <= source < rows_n:
                            sums[row] = sums[row] + rows[source] * tap
            mask = (lax.broadcasted_iota(jnp.int32, (1, LANES), 1) + start < active).astype(
                jnp.float32
            )
            bias = depth_bias[:, lanes].astype(jnp.float32)
            for row in range(rows_n):
                spatial[row, :, lanes] = (sums[row] + bias) * mask
            return carried

        lax.fori_loop(0, channels // LANES, one_chunk, 0)
        inverse = 1.0 / jnp.full((1, 1), active, jnp.int32).astype(jnp.float32)
        gain = ln_gain[...].astype(jnp.float32)
        shift = ln_bias[...].astype(jnp.float32)

        def one_row(row, carried):
            value = spatial[row]
            average = jnp.sum(value, axis=-1, keepdims=True) * inverse
            centred = (value - average) * mask_all
            variance = jnp.sum(centred * centred, axis=-1, keepdims=True) * inverse
            result = (centred * lax.rsqrt(variance + 1e-06) * gain + shift) * mask_all
            normed[slot, pl.ds(pl.multiple_of(row * cols_n, 16), cols_n), :] = result.astype(
                jnp.bfloat16
            )
            return carried

        lax.fori_loop(0, rows_n, one_row, 0)

    def pointwise(slot):
        level = widths[slot]
        active = active_of(level, channels)
        active_hidden = active_of(level, hidden)
        width = 512 if hidden % 512 == 0 else hidden
        total[...] = jnp.zeros_like(total)

        def one_part(part, carried):
            start = pl.multiple_of(part * width, width)
            expanded = lax.dot_general(
                normed[slot],
                in_full[pl.ds(start, width), :],
                (((1,), (1,)), ((), ())),
                preferred_element_type=jnp.float32,
            )
            mask = (lax.broadcasted_iota(jnp.int32, (1, width), 1) + start < active_hidden).astype(
                jnp.float32
            )
            activated = (jax.nn.gelu(expanded, approximate=True) * mask).astype(jnp.bfloat16)
            total[...] += jnp.dot(
                activated, out_full[pl.ds(start, width), :], preferred_element_type=jnp.float32
            )
            return carried

        lax.fori_loop(0, hidden // width, one_part, 0)
        mask_all = (lax.broadcasted_iota(jnp.int32, (1, channels), 1) < active).astype(jnp.float32)
        scale = layer_scale[...].astype(jnp.float32) * mask_all
        for row in range(rows_n):
            value = tiles[slot, row].astype(jnp.float32) * mask_all
            value = value + scale * total[row * cols_n : (row + 1) * cols_n, :]
            results[slot, row] = value.astype(jnp.bfloat16)

    def gather_step(step, carried):
        rightward = chip - step
        leftward = chip + step
        for kind in range(2):
            @pl.when(rightward >= 0)
            def _():
                shard = 2 * rightward + core

                @pl.when(step > 0)
                def _():
                    weight_copy(kind, shard, sibling, 0, step).wait_recv()

                @pl.when(chip + 1 < chips)
                def _():
                    weight_copy(kind, shard, rank + 2, 0, step).start()

            @pl.when(leftward < chips)
            def _():
                shard = 2 * leftward + core

                @pl.when(step > 0)
                def _():
                    weight_copy(kind, shard, sibling, 1, step).wait_recv()

                @pl.when(chip > 0)
                def _():
                    weight_copy(kind, shard, rank - 2, 1, step).start()

                @pl.when(step > 0)
                def _():
                    weight_copy(kind, shard, sibling, 3, step).start()

            @pl.when(rightward >= 0)
            def _():
                weight_copy(kind, 2 * rightward + core, sibling, 2, step).start()

        @pl.when((position == 0) & (step < count))
        def _():
            conv_norm((step + halfway) % count)

        return carried

    lax.fori_loop(0, chips, gather_step, 0)

    def siblings_in(other, carried):
        for kind in range(2):
            weight_copy(kind, 2 * other + 1 - core, sibling, 0, 0).wait_recv()
        return carried

    lax.fori_loop(0, chips, siblings_in, 0)

    def forward(slot):
        return pltpu.make_async_remote_copy(
            src_ref=results.at[slot],
            dst_ref=tiles.at[slot],
            send_sem=tile_send.at[slot],
            recv_sem=tile_recv.at[slot],
            device_id={"section": position + 1},
            device_id_type=MESH,
        )

    def incoming(slot):
        return pltpu.make_async_remote_copy(
            src_ref=results.at[slot],
            dst_ref=tiles.at[slot],
            send_sem=tile_send.at[slot],
            recv_sem=tile_recv.at[slot],
            device_id={"section": mirror},
            device_id_type=MESH,
        )

    def across(slot):
        return pltpu.make_async_remote_copy(
            src_ref=results.at[slot],
            dst_ref=out.at[slot],
            send_sem=store_send.at[slot],
            recv_sem=store_recv.at[slot],
            device_id={"section": mirror},
            device_id_type=MESH,
        )

    def one_slot(index, carried):
        slot = (index + halfway) % count

        @pl.when(position > 0)
        def _():
            incoming(slot).wait_recv()

        @pl.when((position > 0) | (index >= chips))
        def _():
            conv_norm(slot)

        pointwise(slot)

        @pl.when(position + 1 < sections)
        def _():
            forward(slot).start()

        @pl.when(slot >= halfway)
        def _():
            across(slot).start()

        @pl.when(slot < halfway)
        def _():
            out[slot] = results[slot]

        return carried

    lax.fori_loop(0, count, one_slot, 0)

    def drain_weights(step, carried):
        for kind in range(2):
            @pl.when(chip - step >= 0)
            def _():
                shard = 2 * (chip - step) + core

                @pl.when(chip + 1 < chips)
                def _():
                    weight_copy(kind, shard, rank + 2, 0, step).wait_send()

                weight_copy(kind, shard, sibling, 2, step).wait_send()

            @pl.when(chip + step < chips)
            def _():
                shard = 2 * (chip + step) + core

                @pl.when(chip > 0)
                def _():
                    weight_copy(kind, shard, rank - 2, 1, step).wait_send()

                @pl.when(step > 0)
                def _():
                    weight_copy(kind, shard, sibling, 3, step).wait_send()

        return carried

    lax.fori_loop(0, chips, drain_weights, 0)

    for slot in range(count):
        @pl.when(position + 1 < sections)
        def _():
            forward(slot).wait_send()

        if slot >= halfway:
            across(slot).wait_send()
            across(slot).wait_recv()


def on_device(sections, shards, images, widths, *parameters):
    depth_kernel, depth_bias, ln_gain, ln_bias, w_in, w_out, layer_scale = parameters
    count, _, rows_n, cols_n, channels = images.shape
    side = depth_kernel.shape[1]
    hidden = w_in.shape[1] * shards
    tile = (count, rows_n, cols_n, channels)
    vmem = pl.BlockSpec(memory_space=pltpu.VMEM)
    anywhere = pl.BlockSpec(memory_space=pl.ANY)
    stored = pl.pallas_call(
        functools.partial(relay_kernel, sections, shards),
        out_shape=jax.ShapeDtypeStruct(tile, jnp.bfloat16),
        in_specs=[
            pl.BlockSpec(memory_space=pltpu.SMEM),
            anywhere,
            vmem,
            vmem,
            vmem,
            vmem,
            anywhere,
            anywhere,
            vmem,
        ],
        out_specs=vmem,
        scratch_shapes=[
            pltpu.VMEM((hidden, channels), jnp.bfloat16),
            pltpu.VMEM((hidden, channels), jnp.bfloat16),
            pltpu.VMEM(tile, jnp.bfloat16),
            pltpu.VMEM(tile, jnp.bfloat16),
            pltpu.VMEM((rows_n, cols_n + 2 * LEFT, channels), jnp.float32),
            pltpu.VMEM((rows_n, cols_n, channels), jnp.float32),
            pltpu.VMEM((count, rows_n * cols_n, channels), jnp.bfloat16),
            pltpu.VMEM((rows_n * cols_n, channels), jnp.float32),
            pltpu.VMEM((side, side + 1, channels), jnp.float32),
            pltpu.SemaphoreType.DMA((2,)),
            pltpu.SemaphoreType.DMA((count,)),
            pltpu.SemaphoreType.DMA((2, 4, shards // 2)),
            pltpu.SemaphoreType.DMA((2, shards)),
            pltpu.SemaphoreType.DMA((count,)),
            pltpu.SemaphoreType.DMA((count,)),
            pltpu.SemaphoreType.DMA((count,)),
            pltpu.SemaphoreType.DMA((count,)),
        ],
        compiler_params=pltpu.CompilerParams(collective_id=0, has_side_effects=True),
        name="relay",
    )(
        widths,
        images,
        depth_kernel,
        depth_bias,
        ln_gain,
        ln_bias,
        w_in,
        w_out,
        layer_scale,
    )
    return stored[None, :, None]


def solution(mesh):
    placed = (
        P(None, "dp", None, None, None),
        P(),
        P("section", None, None, None),
        P("section", None),
        P("section", None),
        P("section", None),
        P("section", "dp", None),
        P("section", "dp", None),
        P("section", None),
    )
    return jax.shard_map(
        functools.partial(on_device, mesh.shape["section"], mesh.shape["dp"]),
        mesh=mesh,
        in_specs=placed,
        out_specs=P("section", None, "dp", None, None, None),
        check_vma=False,
    )
```

time: 270 us -> 112 us (0.41)
  waiting for transfers between devices: 165 us -> 0 us
  Pallas kernels: 0 us -> 110 us
  starting transfers between devices: 44.2 us -> 0 us
  other arithmetic: 19.5 us -> 0 us
  matrix products: 14.7 us -> 0 us
  between operations: 13.2 us -> 0.01 us
  loops' own time: 6.28 us -> 0 us
  local copies, waits for them, and re-layouts: 7.06 us -> 2.07 us
    pallas_call x0 -> x1, Pallas kernels: none -> 110 us  [on_device(): pl.pallas_call(functools.partial(relay_kernel, sections, shards), out_sha...]
    ppermute x24 -> x0, waiting for transfers between devices: 81.8 us -> none  [the longest x10 48.6 us: passed_along(): lax.ppermute(value, axis, [(source, source + steps) for source in range(i...]
    all_gather x4 -> x0, waiting for transfers between devices: 81.4 us -> none  [the longest x1 32.4 us: on_device(): lax.all_gather(shards[0], 'dp', axis=1, tiled=True)]
    ppermute x24 -> x0, starting transfers between devices: 44 us -> none  [the longest x10 32.6 us: passed_along(): lax.ppermute(value, axis, [(source, source + steps) for source in range(i...]
    dot_general x4 -> x0, matrix products: 14.7 us -> none  [conv_block(): jnp.dot(activated, w_out, preferred_element_type=jnp.float32)]
    reduce_sum x8 -> x0, other arithmetic: 14.7 us -> none  [the longest x4 13.8 us: conv_block(): average = jnp.sum(spatial, axis=-1, keepdims=True) / channel_count]
    another operation x11 -> x0, loops' own time: 6.28 us -> none  [the longest x10 5.86 us: run_slot(): lax.cond(is_live, lambda operand: conv_block(operand, width_level, *param...]
    dynamic_slice x14 -> x0, local copies, waits for them, and re-layouts: 2.86 us -> none  [the longest x4 2.63 us: run_slot(): width_level = widths[clipped]]
  transfers between devices with their start and end apart: 28 -> 0, of which waited for: 17 -> 0; matrix products, arithmetic and copies ran while one was open for 8% -> 0% of each run, Pallas kernels for 0% -> 0%
where the time goes in v1:
time: 112 us
  Pallas kernels  110 us (98%)
  local copies, waits for them, and re-layouts  2.07 us (2%)
    pallas_call x1, Pallas kernels, on_device(): pl.pallas_call(functools.partial(relay_kernel, sections, shards), out_sha...  110 us

profile of v1, /device:TPU:6, one launch (start us, length us, event | category | flops | bytes accessed | tf_op | source)
XLA Modules:
  0.0 112.1 jit_solution(18270293738181950271)
XLA Ops:
  0.0 110.1 %relay.1 = bf16[4,8,16,768]{3,2,1,0:T(8,128)(2,1)} custom-call(s32[4]{0:T(128)} %widths.1, bf16[4,1,8,16,768]{4,3,2,1,0:T(8,128)(2,1)} %images.1, bf16[1,7,7,768]{3,2,1,0:T(8,128)(2,1)} %depth_kernel.1, bf16[1,768]{1,0:T(2,128)(2,1)} %depth_bias.1, bf16[1,768]{1,0:T(2,128)(2,1)} %ln_gain.1, bf16[1,768]{1,0:T(2,128)(2,1)} %ln_bias.1, ...), custom_call_target="tpu_custom_call" | custom-call | tf_op jit(solution)/shard_map/relay/pallas_call | solution.py:367
  110.1 2.1 %copy.12 = bf16[1,4,1,8,16,768]{5,4,3,2,1,0:T(8,128)(2,1)} copy(bf16[1,4,1,8,16,768]{5,4,3,2,1,0:T(8,128)(2,1)} %bitcast.3) | data formatting | bytes 1572864

commit v2 on v1

--- a/solution.py
+++ b/solution.py
@@ -10,10 +10,15 @@
 MESH = pl.DeviceIdType.MESH
 LANES = 128
 LEFT = 8
-
-
-def active_of(level, full):
-    return jnp.where(level == 0, full, jnp.where(level == 1, full // 2, full // 4))
+PART = 256
+
+
+def active_of(slot, full):
+    return jnp.where(slot < 2, full, jnp.where(slot == 2, full // 2, full // 4))
+
+
+def pieces_of(slot, full, width):
+    return (active_of(slot, full) + width - 1) // width
 
 
 def relay_kernel(
@@ -33,10 +38,13 @@
     out_full,
     tiles,
     results,
+    staged,
+    remote,
     padded,
     spatial,
     normed,
     total,
+    activated,
     taps,
     local_sem,
     tile_sem,
@@ -55,7 +63,6 @@
     sibling = rank + 1 - 2 * core
     mirror = sections - 1 - position
     count, rows_n, cols_n, channels = tiles.shape
-    halfway = count // 2
     hidden = in_full.shape[0]
     piece = hidden // shards
     side = depth_kernel.shape[1]
@@ -72,13 +79,30 @@
     for copy in own:
         copy.start()
 
+    full_low = jnp.where(widths[0] == 0, 0, 1)
+    full_high = jnp.where(widths[2] == 0, 2, 3)
+    half_low = jnp.where(widths[0] == 0, widths[1], widths[0]) == 1
+    small_low = 1 - full_low
+    small_high = 5 - full_high
+    order = (
+        full_high,
+        full_low,
+        jnp.where(half_low, small_low, small_high),
+        jnp.where(half_low, small_high, small_low),
+    )
+
     def tile_in(slot):
-        return pltpu.make_async_copy(images.at[slot, 0], tiles.at[slot], tile_sem.at[slot])
+        return pltpu.make_async_copy(images.at[slot, 0], staged.at[slot], tile_sem.at[slot])
 
     @pl.when(position == 0)
     def _():
         for slot in range(count):
             tile_in(slot).start()
+
+    for slot in range(1, count):
+        for row in range(rows_n):
+            results[slot, row] = jnp.zeros((cols_n, channels), jnp.bfloat16)
+            remote[slot, row] = jnp.zeros((cols_n, channels), jnp.bfloat16)
 
     barrier = pltpu.get_barrier_semaphore()
     pl.semaphore_signal(barrier, inc=1, device_id={"dp": sibling}, device_id_type=MESH)
@@ -116,6 +140,8 @@
     def _():
         for slot in range(count):
             tile_in(slot).wait()
+        for slot in range(count):
+            tiles[slot] = staged[order[slot]]
 
     def weight_copy(kind, shard, target, lane, step):
         return pltpu.make_async_remote_copy(
@@ -128,17 +154,24 @@
         )
 
     def conv_norm(slot):
-        level = widths[slot]
-        active = active_of(level, channels)
+        active = active_of(slot, channels)
         mask_all = (lax.broadcasted_iota(jnp.int32, (1, channels), 1) < active).astype(jnp.float32)
-        for row in range(rows_n):
-            padded[row, LEFT : LEFT + cols_n, :] = (
-                tiles[slot, row].astype(jnp.float32) * mask_all
-            )
 
         def one_chunk(chunk, carried):
             start = pl.multiple_of(chunk * LANES, LANES)
             lanes = pl.ds(start, LANES)
+            mask = (lax.broadcasted_iota(jnp.int32, (1, LANES), 1) + start < active).astype(
+                jnp.float32
+            )
+
+            @pl.when((position > 0) & (chunk % (PART // LANES) == 0))
+            def _():
+                forward(slot, chunk // (PART // LANES), mirror).wait_recv()
+
+            for row in range(rows_n):
+                padded[row, LEFT : LEFT + cols_n, lanes] = (
+                    tiles[slot, row, :, lanes].astype(jnp.float32) * mask
+                )
             sums = [jnp.zeros((cols_n, LANES), jnp.float32) for _ in range(rows_n)]
             for col in range(side):
                 rows = [
@@ -150,21 +183,20 @@
                         source = row + row_off - reach
                         if 0 <= source < rows_n:
                             sums[row] = sums[row] + rows[source] * tap
-            mask = (lax.broadcasted_iota(jnp.int32, (1, LANES), 1) + start < active).astype(
-                jnp.float32
-            )
             bias = depth_bias[:, lanes].astype(jnp.float32)
             for row in range(rows_n):
                 spatial[row, :, lanes] = (sums[row] + bias) * mask
             return carried
 
-        lax.fori_loop(0, channels // LANES, one_chunk, 0)
+        lax.fori_loop(
+            0, pieces_of(slot, channels, PART) * (PART // LANES), one_chunk, 0
+        )
         inverse = 1.0 / jnp.full((1, 1), active, jnp.int32).astype(jnp.float32)
         gain = ln_gain[...].astype(jnp.float32)
         shift = ln_bias[...].astype(jnp.float32)
 
         def one_row(row, carried):
-            value = spatial[row]
+            value = spatial[row] * mask_all
             average = jnp.sum(value, axis=-1, keepdims=True) * inverse
             centred = (value - average) * mask_all
             variance = jnp.sum(centred * centred, axis=-1, keepdims=True) * inverse
@@ -176,37 +208,107 @@
 
         lax.fori_loop(0, rows_n, one_row, 0)
 
-    def pointwise(slot):
-        level = widths[slot]
-        active = active_of(level, channels)
-        active_hidden = active_of(level, hidden)
-        width = 512 if hidden % 512 == 0 else hidden
-        total[...] = jnp.zeros_like(total)
-
+    def expand(slot, start, width):
+        expanded = lax.dot_general(
+            normed[slot],
+            in_full[pl.ds(start, width), :],
+            (((1,), (1,)), ((), ())),
+            preferred_element_type=jnp.float32,
+        )
+        mask = (
+            lax.broadcasted_iota(jnp.int32, (1, width), 1) + start < active_of(slot, hidden)
+        ).astype(jnp.float32)
+        return (jax.nn.gelu(expanded, approximate=True) * mask).astype(jnp.bfloat16)
+
+    def add_chip(other):
+        start = pl.multiple_of(other * 2 * piece, 2 * piece)
+
+        def one_slot(slot, carried):
+            @pl.when(start < active_of(slot, hidden))
+            def _():
+                total[slot] += jnp.dot(
+                    expand(slot, start, 2 * piece),
+                    out_full[pl.ds(start, 2 * piece), :],
+                    preferred_element_type=jnp.float32,
+                )
+
+            return carried
+
+        lax.fori_loop(0, count, one_slot, 0)
+
+    width = 512 if hidden % 512 == 0 else hidden
+
+    def activate(slot):
         def one_part(part, carried):
             start = pl.multiple_of(part * width, width)
-            expanded = lax.dot_general(
-                normed[slot],
-                in_full[pl.ds(start, width), :],
-                (((1,), (1,)), ((), ())),
+            activated[:, pl.ds(start, width)] = expand(slot, start, width)
+            return carried
+
+        lax.fori_loop(0, pieces_of(slot, hidden, width), one_part, 0)
+
+    def project(slot, part):
+        lanes = pl.ds(pl.multiple_of(part * PART, PART), PART)
+
+        def one_part(index, carried):
+            start = pl.multiple_of(index * width, width)
+            return carried + jnp.dot(
+                activated[:, pl.ds(start, width)],
+                out_full[pl.ds(start, width), lanes],
                 preferred_element_type=jnp.float32,
             )
-            mask = (lax.broadcasted_iota(jnp.int32, (1, width), 1) + start < active_hidden).astype(
-                jnp.float32
-            )
-            activated = (jax.nn.gelu(expanded, approximate=True) * mask).astype(jnp.bfloat16)
-            total[...] += jnp.dot(
-                activated, out_full[pl.ds(start, width), :], preferred_element_type=jnp.float32
-            )
+
+        total[slot, :, lanes] = lax.fori_loop(
+            0,
+            pieces_of(slot, hidden, width),
+            one_part,
+            jnp.zeros((rows_n * cols_n, PART), jnp.float32),
+        )
+
+    def finish(slot, part):
+        start = pl.multiple_of(part * PART, PART)
+        lanes = pl.ds(start, PART)
+        mask = (
+            lax.broadcasted_iota(jnp.int32, (1, PART), 1) + start < active_of(slot, channels)
+        ).astype(jnp.float32)
+        scale = layer_scale[:, lanes].astype(jnp.float32) * mask
+        for row in range(rows_n):
+            value = tiles[slot, row, :, lanes].astype(jnp.float32) * mask
+            value = value + scale * total[slot, row * cols_n : (row + 1) * cols_n, lanes]
+            results[slot, row, :, lanes] = value.astype(jnp.bfloat16)
+
+    def forward(slot, part, target):
+        lanes = pl.ds(pl.multiple_of(part * PART, PART), PART)
+        return pltpu.make_async_remote_copy(
+            src_ref=results.at[slot, :, :, lanes],
+            dst_ref=tiles.at[slot, :, :, lanes],
+            send_sem=tile_send.at[slot, part],
+            recv_sem=tile_recv.at[slot, part],
+            device_id={"section": target},
+            device_id_type=MESH,
+        )
+
+    def across(slot, part):
+        lanes = pl.ds(pl.multiple_of(part * PART, PART), PART)
+        return pltpu.make_async_remote_copy(
+            src_ref=results.at[slot, :, :, lanes],
+            dst_ref=remote.at[slot, :, :, lanes],
+            send_sem=store_send.at[slot, part],
+            recv_sem=store_recv.at[slot, part],
+            device_id={"section": mirror},
+            device_id_type=MESH,
+        )
+
+    def each_part(slot, act):
+        def one(part, carried):
+            act(part)
             return carried
 
-        lax.fori_loop(0, hidden // width, one_part, 0)
-        mask_all = (lax.broadcasted_iota(jnp.int32, (1, channels), 1) < active).astype(jnp.float32)
-        scale = layer_scale[...].astype(jnp.float32) * mask_all
-        for row in range(rows_n):
-            value = tiles[slot, row].astype(jnp.float32) * mask_all
-            value = value + scale * total[row * cols_n : (row + 1) * cols_n, :]
-            results[slot, row] = value.astype(jnp.bfloat16)
+        lax.fori_loop(0, pieces_of(slot, channels, PART), one, 0)
+
+    def norm_slot(slot, carried):
+        total[slot] = jnp.zeros(total.shape[1:], jnp.float32)
+        conv_norm(slot)
+        return carried
 
     def gather_step(step, carried):
         rightward = chip - step
@@ -244,75 +346,56 @@
             def _():
                 weight_copy(kind, 2 * rightward + core, sibling, 2, step).start()
 
-        @pl.when((position == 0) & (step < count))
-        def _():
-            conv_norm((step + halfway) % count)
+        def siblings_in(other):
+            for kind in range(2):
+                weight_copy(kind, 2 * other + 1 - core, sibling, 0, 0).wait_recv()
+
+        @pl.when((position == 0) & (step == 0))
+        def _():
+            lax.fori_loop(0, count, norm_slot, 0)
+
+        @pl.when(rightward >= 0)
+        def _():
+            siblings_in(rightward)
+
+            @pl.when(position == 0)
+            def _():
+                add_chip(rightward)
+
+        @pl.when((leftward < chips) & (step > 0))
+        def _():
+            siblings_in(leftward)
+
+            @pl.when(position == 0)
+            def _():
+                add_chip(leftward)
 
         return carried
 
     lax.fori_loop(0, chips, gather_step, 0)
 
-    def siblings_in(other, carried):
-        for kind in range(2):
-            weight_copy(kind, 2 * other + 1 - core, sibling, 0, 0).wait_recv()
-        return carried
-
-    lax.fori_loop(0, chips, siblings_in, 0)
-
-    def forward(slot):
-        return pltpu.make_async_remote_copy(
-            src_ref=results.at[slot],
-            dst_ref=tiles.at[slot],
-            send_sem=tile_send.at[slot],
-            recv_sem=tile_recv.at[slot],
-            device_id={"section": position + 1},
-            device_id_type=MESH,
-        )
-
-    def incoming(slot):
-        return pltpu.make_async_remote_copy(
-            src_ref=results.at[slot],
-            dst_ref=tiles.at[slot],
-            send_sem=tile_send.at[slot],
-            recv_sem=tile_recv.at[slot],
-            device_id={"section": mirror},
-            device_id_type=MESH,
-        )
-
-    def across(slot):
-        return pltpu.make_async_remote_copy(
-            src_ref=results.at[slot],
-            dst_ref=out.at[slot],
-            send_sem=store_send.at[slot],
-            recv_sem=store_recv.at[slot],
-            device_id={"section": mirror},
-            device_id_type=MESH,
-        )
-
-    def one_slot(index, carried):
-        slot = (index + halfway) % count
-
+    def one_slot(slot, carried):
         @pl.when(position > 0)
         def _():
-            incoming(slot).wait_recv()
-
-        @pl.when((position > 0) | (index >= chips))
-        def _():
             conv_norm(slot)
-
-        pointwise(slot)
-
-        @pl.when(position + 1 < sections)
-        def _():
-            forward(slot).start()
-
-        @pl.when(slot >= halfway)
-        def _():
-            across(slot).start()
-
-        @pl.when(slot < halfway)
-        def _():
-            out[slot] = results[slot]
+            activate(slot)
+
+        def one_part(part):
+            @pl.when(position > 0)
+            def _():
+                project(slot, part)
+
+            finish(slot, part)
+
+            @pl.when(position + 1 < sections)
+            def _():
+                forward(slot, part, position + 1).start()
+
+        each_part(slot, one_part)
+
+        @pl.when(slot != 1)
+        def _():
+            each_part(slot, lambda part: across(slot, part).start())
 
         return carried
 
@@ -346,14 +429,24 @@
 
     lax.fori_loop(0, chips, drain_weights, 0)
 
-    for slot in range(count):
+    out[0] = results[jnp.where(full_low == 0, 1, jnp.where(half_low, 2, 3))]
+    out[1] = results[jnp.where(full_low == 1, 1, jnp.where(half_low, 2, 3))]
+
+    def drain_slot(slot, carried):
         @pl.when(position + 1 < sections)
         def _():
-            forward(slot).wait_send()
-
-        if slot >= halfway:
-            across(slot).wait_send()
-            across(slot).wait_recv()
+            each_part(slot, lambda part: forward(slot, part, mirror).wait_send())
+
+        @pl.when(slot != 1)
+        def _():
+            each_part(slot, lambda part: across(slot, part).wait_send())
+            each_part(slot, lambda part: across(slot, part).wait_recv())
+
+        return carried
+
+    lax.fori_loop(0, count, drain_slot, 0)
+    out[2] = remote[jnp.where(full_high == 2, 0, jnp.where(half_low, 3, 2))]
+    out[3] = remote[jnp.where(full_high == 3, 0, jnp.where(half_low, 3, 2))]
 
 
 def on_device(sections, shards, images, widths, *parameters):
@@ -384,19 +477,22 @@
             pltpu.VMEM((hidden, channels), jnp.bfloat16),
             pltpu.VMEM(tile, jnp.bfloat16),
             pltpu.VMEM(tile, jnp.bfloat16),
+            pltpu.VMEM(tile, jnp.bfloat16),
+            pltpu.VMEM(tile, jnp.bfloat16),
             pltpu.VMEM((rows_n, cols_n + 2 * LEFT, channels), jnp.float32),
             pltpu.VMEM((rows_n, cols_n, channels), jnp.float32),
             pltpu.VMEM((count, rows_n * cols_n, channels), jnp.bfloat16),
-            pltpu.VMEM((rows_n * cols_n, channels), jnp.float32),
+            pltpu.VMEM((count, rows_n * cols_n, channels), jnp.float32),
+            pltpu.VMEM((rows_n * cols_n, hidden), jnp.bfloat16),
             pltpu.VMEM((side, side + 1, channels), jnp.float32),
             pltpu.SemaphoreType.DMA((2,)),
             pltpu.SemaphoreType.DMA((count,)),
             pltpu.SemaphoreType.DMA((2, 4, shards // 2)),
             pltpu.SemaphoreType.DMA((2, shards)),
-            pltpu.SemaphoreType.DMA((count,)),
-            pltpu.SemaphoreType.DMA((count,)),
-            pltpu.SemaphoreType.DMA((count,)),
-            pltpu.SemaphoreType.DMA((count,)),
+            pltpu.SemaphoreType.DMA((count, channels // PART)),
+            pltpu.SemaphoreType.DMA((count, channels // PART)),
+            pltpu.SemaphoreType.DMA((count, channels // PART)),
+            pltpu.SemaphoreType.DMA((count, channels // PART)),
         ],
         compiler_params=pltpu.CompilerParams(collective_id=0, has_side_effects=True),
         name="relay",

time: 112 us -> 107 us (0.955)
  the two profiles are of different devices: /device:TPU:6 before, /device:TPU:0 now
where the time goes in v2:
time: 107 us
  Pallas kernels  105 us (98%)
  local copies, waits for them, and re-layouts  2.07 us (2%)
    pallas_call x1, Pallas kernels, on_device(): pl.pallas_call(functools.partial(relay_kernel, sections, shards), out_sha...  105 us

profile of v2, /device:TPU:0, one launch (start us, length us, event | category | flops | bytes accessed | tf_op | source)
XLA Modules:
  0.0 107.1 jit_solution(17544714758355278145)
XLA Ops:
  0.0 105.0 %relay.1 = bf16[4,8,16,768]{3,2,1,0:T(8,128)(2,1)} custom-call(s32[4]{0:T(128)} %widths.1, bf16[4,1,8,16,768]{4,3,2,1,0:T(8,128)(2,1)} %images.1, bf16[1,7,7,768]{3,2,1,0:T(8,128)(2,1)} %depth_kernel.1, bf16[1,768]{1,0:T(2,128)(2,1)} %depth_bias.1, bf16[1,768]{1,0:T(2,128)(2,1)} %ln_gain.1, bf16[1,768]{1,0:T(2,128)(2,1)} %ln_bias.1, ...), custom_call_target="tpu_custom_call" | custom-call | tf_op jit(solution)/shard_map/relay/pallas_call | solution.py:460
  105.0 2.1 %copy.12 = bf16[1,4,1,8,16,768]{5,4,3,2,1,0:T(8,128)(2,1)} copy(bf16[1,4,1,8,16,768]{5,4,3,2,1,0:T(8,128)(2,1)} %bitcast.3) | data formatting | bytes 1572864

commit v3 on v2

--- a/solution.py
+++ b/solution.py
@@ -220,18 +220,20 @@
         ).astype(jnp.float32)
         return (jax.nn.gelu(expanded, approximate=True) * mask).astype(jnp.bfloat16)
 
+    def add_to(slot, start):
+        @pl.when(start < active_of(slot, hidden))
+        def _():
+            total[slot] += jnp.dot(
+                expand(slot, start, 2 * piece),
+                out_full[pl.ds(start, 2 * piece), :],
+                preferred_element_type=jnp.float32,
+            )
+
     def add_chip(other):
         start = pl.multiple_of(other * 2 * piece, 2 * piece)
 
         def one_slot(slot, carried):
-            @pl.when(start < active_of(slot, hidden))
-            def _():
-                total[slot] += jnp.dot(
-                    expand(slot, start, 2 * piece),
-                    out_full[pl.ds(start, 2 * piece), :],
-                    preferred_element_type=jnp.float32,
-                )
-
+            add_to(slot, start)
             return carried
 
         lax.fori_loop(0, count, one_slot, 0)
@@ -310,9 +312,42 @@
         conv_norm(slot)
         return carried
 
+    def siblings_in(other):
+        for kind in range(2):
+            weight_copy(kind, 2 * other + 1 - core, sibling, 0, 0).wait_recv()
+
+    def absorb(step):
+        rightward = chip - step
+        leftward = chip + step
+
+        @pl.when(rightward >= 0)
+        def _():
+            siblings_in(rightward)
+
+            @pl.when(position == 0)
+            def _():
+                add_chip(rightward)
+
+        @pl.when((leftward < chips) & (step > 0))
+        def _():
+            siblings_in(leftward)
+
+            @pl.when(position == 0)
+            def _():
+                add_chip(leftward)
+
     def gather_step(step, carried):
         rightward = chip - step
         leftward = chip + step
+
+        @pl.when((position == 0) & (step == 1))
+        def _():
+            lax.fori_loop(2, count, norm_slot, 0)
+
+        @pl.when(step > 0)
+        def _():
+            absorb(step - 1)
+
         for kind in range(2):
             @pl.when(rightward >= 0)
             def _():
@@ -346,33 +381,20 @@
             def _():
                 weight_copy(kind, 2 * rightward + core, sibling, 2, step).start()
 
-        def siblings_in(other):
-            for kind in range(2):
-                weight_copy(kind, 2 * other + 1 - core, sibling, 0, 0).wait_recv()
-
         @pl.when((position == 0) & (step == 0))
         def _():
-            lax.fori_loop(0, count, norm_slot, 0)
-
-        @pl.when(rightward >= 0)
-        def _():
-            siblings_in(rightward)
-
-            @pl.when(position == 0)
-            def _():
-                add_chip(rightward)
-
-        @pl.when((leftward < chips) & (step > 0))
-        def _():
-            siblings_in(leftward)
-
-            @pl.when(position == 0)
-            def _():
-                add_chip(leftward)
+            lax.fori_loop(0, 2, norm_slot, 0)
 
         return carried
 
     lax.fori_loop(0, chips, gather_step, 0)
+    at_end = (chip == 0) | (chip == chips - 1)
+    far = chips - 1 - chip
+    far_start = pl.multiple_of(far * 2 * piece, 2 * piece)
+
+    @pl.when(at_end)
+    def _():
+        siblings_in(far)
 
     def one_slot(slot, carried):
         @pl.when(position > 0)
@@ -380,6 +402,10 @@
             conv_norm(slot)
             activate(slot)
 
+        @pl.when((position == 0) & at_end)
+        def _():
+            add_to(slot, far_start)
+
         def one_part(part):
             @pl.when(position > 0)
             def _():
@@ -393,13 +419,33 @@
 
         each_part(slot, one_part)
 
-        @pl.when(slot != 1)
+        @pl.when((slot != 1) & (position == sections - 1))
         def _():
             each_part(slot, lambda part: across(slot, part).start())
 
         return carried
 
     lax.fori_loop(0, count, one_slot, 0)
+    sends_across = position != sections // 2 - 1
+    takes_across = position != sections // 2
+
+    def store_slot(slot, carried):
+        @pl.when((slot != 1) & (position < sections - 1) & sends_across)
+        def _():
+            each_part(slot, lambda part: across(slot, part).start())
+
+        def keep(part):
+            lanes = pl.ds(pl.multiple_of(part * PART, PART), PART)
+            for row in range(rows_n):
+                remote[slot, row, :, lanes] = tiles[slot, row, :, lanes]
+
+        @pl.when((slot != 1) & (position == sections // 2))
+        def _():
+            each_part(slot, keep)
+
+        return carried
+
+    lax.fori_loop(0, count, store_slot, 0)
 
     def drain_weights(step, carried):
         for kind in range(2):
@@ -437,9 +483,12 @@
         def _():
             each_part(slot, lambda part: forward(slot, part, mirror).wait_send())
 
-        @pl.when(slot != 1)
+        @pl.when((slot != 1) & sends_across)
         def _():
             each_part(slot, lambda part: across(slot, part).wait_send())
+
+        @pl.when((slot != 1) & takes_across)
+        def _():
             each_part(slot, lambda part: across(slot, part).wait_recv())
 
         return carried

time: 107 us -> 106 us (level)
  Pallas kernels: 105 us -> 103 us
    pallas_call x1, Pallas kernels: 105 us -> 103 us  [on_device(): pl.pallas_call(functools.partial(relay_kernel, sections, shards), out_sha...]
where the time goes in v3:
time: 106 us; the launch traced here: 105 us
  Pallas kernels  103 us (97%)
  local copies, waits for them, and re-layouts  2.07 us (2%)
    pallas_call x1, Pallas kernels, on_device(): pl.pallas_call(functools.partial(relay_kernel, sections, shards), out_sha...  103 us

profile of v3, /device:TPU:0, one launch (start us, length us, event | category | flops | bytes accessed | tf_op | source)
XLA Modules:
  0.0 105.4 jit_solution(15560892759514057791)
XLA Ops:
  0.0 103.3 %relay.1 = bf16[4,8,16,768]{3,2,1,0:T(8,128)(2,1)} custom-call(s32[4]{0:T(128)} %widths.1, bf16[4,1,8,16,768]{4,3,2,1,0:T(8,128)(2,1)} %images.1, bf16[1,7,7,768]{3,2,1,0:T(8,128)(2,1)} %depth_kernel.1, bf16[1,768]{1,0:T(2,128)(2,1)} %depth_bias.1, bf16[1,768]{1,0:T(2,128)(2,1)} %ln_gain.1, bf16[1,768]{1,0:T(2,128)(2,1)} %ln_bias.1, ...), custom_call_target="tpu_custom_call" | custom-call | tf_op jit(solution)/shard_map/relay/pallas_call | solution.py:509
  103.3 2.1 %copy.12 = bf16[1,4,1,8,16,768]{5,4,3,2,1,0:T(8,128)(2,1)} copy(bf16[1,4,1,8,16,768]{5,4,3,2,1,0:T(8,128)(2,1)} %bitcast.3) | data formatting | bytes 1572864

commit v4 on v3

--- a/solution.py
+++ b/solution.py
@@ -11,6 +11,7 @@
 LANES = 128
 LEFT = 8
 PART = 256
+SUB = 8
 
 
 def active_of(slot, full):
@@ -118,10 +119,21 @@
     greet(position + 1 < sections, {"section": position + 1})
     greet(position > 0, {"section": position - 1})
 
-    for row in range(side):
-        taps[row, 0:side, :] = depth_kernel[0, row].astype(jnp.float32)
-    padded[:, 0:LEFT, :] = jnp.zeros((rows_n, LEFT, channels), jnp.float32)
-    padded[:, LEFT + cols_n :, :] = jnp.zeros((rows_n, LEFT, channels), jnp.float32)
+    for row in range(rows_n):
+        padded[row, 0:LEFT, :] = jnp.zeros((LEFT, LANES), jnp.float32)
+        padded[row, LEFT + cols_n :, :] = jnp.zeros((LEFT, LANES), jnp.float32)
+
+    def spread(chunk, carried):
+        lanes = pl.ds(pl.multiple_of(chunk * LANES, LANES), LANES)
+        for row in range(side):
+            strip = depth_kernel[0, row, :, lanes].astype(jnp.float32)
+            for col in range(side):
+                taps[chunk, row * side + col] = jnp.broadcast_to(
+                    strip[col : col + 1, :], (SUB, LANES)
+                )
+        return carried
+
+    lax.fori_loop(0, channels // LANES, spread, 0)
     for copy in own:
         copy.wait()
 
@@ -169,23 +181,30 @@
                 forward(slot, chunk // (PART // LANES), mirror).wait_recv()
 
             for row in range(rows_n):
-                padded[row, LEFT : LEFT + cols_n, lanes] = (
+                padded[row, LEFT : LEFT + cols_n, :] = (
                     tiles[slot, row, :, lanes].astype(jnp.float32) * mask
                 )
-            sums = [jnp.zeros((cols_n, LANES), jnp.float32) for _ in range(rows_n)]
+            halves = range(cols_n // SUB)
+            bias = jnp.broadcast_to(depth_bias[:, lanes].astype(jnp.float32), (SUB, LANES))
+            sums = [[bias for _ in halves] for _ in range(rows_n)]
             for col in range(side):
                 rows = [
-                    padded[row, pl.ds(LEFT - reach + col, cols_n), lanes] for row in range(rows_n)
+                    [
+                        padded[row, pl.ds(LEFT - reach + col + SUB * half, SUB), :]
+                        for half in halves
+                    ]
+                    for row in range(rows_n)
                 ]
                 for row_off in range(side):
-                    tap = taps[row_off, pl.ds(col, 1), lanes]
+                    tap = taps[chunk, row_off * side + col]
                     for row in range(rows_n):
                         source = row + row_off - reach
                         if 0 <= source < rows_n:
-                            sums[row] = sums[row] + rows[source] * tap
-            bias = depth_bias[:, lanes].astype(jnp.float32)
+                            for half in halves:
+                                sums[row][half] = sums[row][half] + rows[source][half] * tap
             for row in range(rows_n):
-                spatial[row, :, lanes] = (sums[row] + bias) * mask
+                for half in halves:
+                    spatial[row, SUB * half : SUB * (half + 1), lanes] = sums[row][half] * mask
             return carried
 
         lax.fori_loop(
@@ -201,12 +220,13 @@
             centred = (value - average) * mask_all
             variance = jnp.sum(centred * centred, axis=-1, keepdims=True) * inverse
             result = (centred * lax.rsqrt(variance + 1e-06) * gain + shift) * mask_all
-            normed[slot, pl.ds(pl.multiple_of(row * cols_n, 16), cols_n), :] = result.astype(
+            normed[slot, row * cols_n : (row + 1) * cols_n, :] = result.astype(
                 jnp.bfloat16
             )
             return carried
 
-        lax.fori_loop(0, rows_n, one_row, 0)
+        for row in range(rows_n):
+            one_row(row, 0)
 
     def expand(slot, start, width):
         expanded = lax.dot_general(
@@ -528,12 +548,12 @@
             pltpu.VMEM(tile, jnp.bfloat16),
             pltpu.VMEM(tile, jnp.bfloat16),
             pltpu.VMEM(tile, jnp.bfloat16),
-            pltpu.VMEM((rows_n, cols_n + 2 * LEFT, channels), jnp.float32),
+            pltpu.VMEM((rows_n, cols_n + 2 * LEFT, LANES), jnp.float32),
             pltpu.VMEM((rows_n, cols_n, channels), jnp.float32),
             pltpu.VMEM((count, rows_n * cols_n, channels), jnp.bfloat16),
             pltpu.VMEM((count, rows_n * cols_n, channels), jnp.float32),
             pltpu.VMEM((rows_n * cols_n, hidden), jnp.bfloat16),
-            pltpu.VMEM((side, side + 1, channels), jnp.float32),
+            pltpu.VMEM((channels // LANES, side * side, SUB, LANES), jnp.float32),
             pltpu.SemaphoreType.DMA((2,)),
             pltpu.SemaphoreType.DMA((count,)),
             pltpu.SemaphoreType.DMA((2, 4, shards // 2)),

time: 106 us -> 92.2 us (0.87)
  Pallas kernels: 103 us -> 89.9 us
    pallas_call x1, Pallas kernels: 103 us -> 89.9 us  [on_device(): pl.pallas_call(functools.partial(relay_kernel, sections, shards), out_sha...]
where the time goes in v4:
time: 92.2 us; the launch traced here: 92 us
  Pallas kernels  89.9 us (98%)
  local copies, waits for them, and re-layouts  2.07 us (2%)
    pallas_call x1, Pallas kernels, on_device(): pl.pallas_call(functools.partial(relay_kernel, sections, shards), out_sha...  89.9 us
    unnamed x1, local copies, waits for them, and re-layouts  2.07 us

profile of v4, /device:TPU:0, one launch (start us, length us, event | category | flops | bytes accessed | tf_op | source)
XLA Modules:
  0.0 92.0 jit_solution(6097859305787368300)
XLA Ops:
  0.0 89.9 %relay.1 = bf16[4,8,16,768]{3,2,1,0:T(8,128)(2,1)} custom-call(s32[4]{0:T(128)} %widths.1, bf16[4,1,8,16,768]{4,3,2,1,0:T(8,128)(2,1)} %images.1, bf16[1,7,7,768]{3,2,1,0:T(8,128)(2,1)} %depth_kernel.1, bf16[1,768]{1,0:T(2,128)(2,1)} %depth_bias.1, bf16[1,768]{1,0:T(2,128)(2,1)} %ln_gain.1, bf16[1,768]{1,0:T(2,128)(2,1)} %ln_bias.1, ...), custom_call_target="tpu_custom_call" | custom-call | tf_op jit(solution)/shard_map/relay/pallas_call | solution.py:529
  89.9 2.1 %copy.12 = bf16[1,4,1,8,16,768]{5,4,3,2,1,0:T(8,128)(2,1)} copy(bf16[1,4,1,8,16,768]{5,4,3,2,1,0:T(8,128)(2,1)} %bitcast.3) | data formatting | bytes 1572864

commit v5 on v4

--- a/solution.py
+++ b/solution.py
@@ -416,6 +416,10 @@
     def _():
         siblings_in(far)
 
+    inner = (position > 0) & (position < sections - 1)
+    sends_across = position != sections // 2 - 1
+    takes_across = position != sections // 2
+
     def one_slot(slot, carried):
         @pl.when(position > 0)
         def _():
@@ -443,14 +447,18 @@
         def _():
             each_part(slot, lambda part: across(slot, part).start())
 
+        @pl.when((slot == 2) & inner & sends_across)
+        def _():
+            each_part(0, lambda part: across(0, part).start())
+
         return carried
 
     lax.fori_loop(0, count, one_slot, 0)
-    sends_across = position != sections // 2 - 1
-    takes_across = position != sections // 2
 
     def store_slot(slot, carried):
-        @pl.when((slot != 1) & (position < sections - 1) & sends_across)
+        early = (slot == 0) & inner
+
+        @pl.when((slot != 1) & (position < sections - 1) & sends_across & ~early)
         def _():
             each_part(slot, lambda part: across(slot, part).start())
 

time: 92.2 us -> 92.2 us (level)
  no operation moved by 1% of the time
where the time goes in v5:
time: 92.2 us; the launch traced here: 92 us
  Pallas kernels  90 us (98%)
  local copies, waits for them, and re-layouts  2.07 us (2%)
    pallas_call x1, Pallas kernels, on_device(): pl.pallas_call(functools.partial(relay_kernel, sections, shards), out_sha...  90 us
    unnamed x1, local copies, waits for them, and re-layouts  2.07 us

profile of v5, /device:TPU:0, one launch (start us, length us, event | category | flops | bytes accessed | tf_op | source)
XLA Modules:
  0.0 92.0 jit_solution(4764259439674214443)
XLA Ops:
  0.0 90.0 %relay.1 = bf16[4,8,16,768]{3,2,1,0:T(8,128)(2,1)} custom-call(s32[4]{0:T(128)} %widths.1, bf16[4,1,8,16,768]{4,3,2,1,0:T(8,128)(2,1)} %images.1, bf16[1,7,7,768]{3,2,1,0:T(8,128)(2,1)} %depth_kernel.1, bf16[1,768]{1,0:T(2,128)(2,1)} %depth_bias.1, bf16[1,768]{1,0:T(2,128)(2,1)} %ln_gain.1, bf16[1,768]{1,0:T(2,128)(2,1)} %ln_bias.1, ...), custom_call_target="tpu_custom_call" | custom-call | tf_op jit(solution)/shard_map/relay/pallas_call | solution.py:537
  90.0 2.1 %copy.12 = bf16[1,4,1,8,16,768]{5,4,3,2,1,0:T(8,128)(2,1)} copy(bf16[1,4,1,8,16,768]{5,4,3,2,1,0:T(8,128)(2,1)} %bitcast.3) | data formatting | bytes 1572864
